TPU v7x, 32 devices: a whole 2x2x4 slice. The times are simulated.
32 devices in a mesh: dp: 8 (over y, x, core), mp: 4 (over z).
Axes of the slice: x: 2, y: 2, z: 4, core: 2. Of those that a mesh axis runs over, the one named last changes fastest.
Arguments:
- tokens: bfloat16 [11264, 768], P('dp'), may hold values from -6 to 6
- lang: int32 [16], P('dp'), may hold values from 0 to 7
- page_len: int32 [16], P('dp'), may hold values from 374 to 561, as said below
- rel_pos: int32 [16, 704, 704], P('dp', 'mp'), may hold values from 0 to 31, as said below
- rel_x: int32 [16, 704, 704], P('dp', 'mp'), may hold values from 0 to 63, as said below
- rel_y: int32 [16, 704, 704], P('dp', 'mp'), may hold values from 0 to 63, as said below
- lang_table: float32 [8, 768], replicated, may hold values from -3 to 3
- convolution_weight: float32 [3, 768], replicated, may hold values from -2.4 to 2.4
- conv_b: float32 [768], replicated, may hold values from -1.8 to 1.8
- w_qkv: bfloat16 [768, 3, 768], P(None, None, 'mp'), may hold values from -0.21875 to 0.21875
- b_qv: float32 [2, 768], P(None, 'mp'), may hold values from -1.8 to 1.8
- bias_table: float32 [160, 12], replicated, may hold values from -3 to 3
- w_out: bfloat16 [768, 768], P('mp'), may hold values from -1.5 to 1.5
- b_out: float32 [768], replicated, may hold values from -1.8 to 1.8
- ln1_gain: float32 [768], replicated, may hold values from 0.5 to 1.5
- ln1_bias: float32 [768], replicated, may hold values from -1.8 to 1.8
- w_in: bfloat16 [768, 3072], P(None, 'mp'), may hold values from -0.21875 to 0.21875
- b_in: float32 [3072], P('mp'), may hold values from -1.8 to 1.8
- w_down: bfloat16 [3072, 768], P('mp'), may hold values from -0.109375 to 0.109375
- b_down: float32 [768], replicated, may hold values from -1.8 to 1.8
- ln2_gain: float32 [768], replicated, may hold values from 0.5 to 1.5
- ln2_bias: float32 [768], replicated, may hold values from -1.8 to 1.8
- cotangent: bfloat16 [11264, 768], P('dp'), may hold values from -6 to 6
Outputs:
- out: bfloat16 [11264, 768], P('dp')
- d_tokens: bfloat16 [11264, 768], P('dp')
- d_lang_table: float32 [8, 768], replicated
- d_conv_w: float32 [3, 768], replicated
- d_conv_b: float32 [768], replicated
- d_w_qkv: float32 [768, 3, 768], P(None, None, 'mp')
- d_b_qv: float32 [2, 768], P(None, 'mp')
- d_bias_table: float32 [160, 12], replicated
- d_w_out: float32 [768, 768], P('mp')
- d_b_out: float32 [768], replicated
- d_ln1_gain: float32 [768], replicated
- d_ln1_bias: float32 [768], replicated
- d_w_in: float32 [768, 3072], P(None, 'mp')
- d_b_in: float32 [3072], P('mp')
- d_w_down: float32 [3072, 768], P('mp')
- d_b_down: float32 [768], replicated
- d_ln2_gain: float32 [768], replicated
- d_ln2_bias: float32 [768], replicated
Inputs may be any that keep to these rules, and one draw needn't show every extreme that they name: `page_len`: the live tokens of a page fill its first slots; one page has exactly 561. `rel_pos`: bucket of the key's reading position minus the query's; positive offsets take the upper 32 // 2 buckets. `rel_x`: bucket of the key's horizontal coordinate minus the query's; positive offsets take the upper 64 // 2 buckets. `rel_y`: bucket of the key's vertical coordinate minus the query's; positive offsets take the upper 64 // 2 buckets.
All inputs are finite; a program needn't handle non-finite values.
Results may differ from a plain program's by a relative error of at most 0.02.
The roundings to bfloat16 on the way count: a program that leaves them out, or rounds other values in their place, can miss the bound.
Values may be sent and summed in bfloat16 or wider, within the bound.
No kernel may reach another device: no remote copies, remote signals or barrier semaphores. Data moves between devices by JAX's collectives and lax.ppermute only.
A program may use at most 256 MiB of HBM per device.

v0:
```python
import math
import jax
import jax.numpy as jnp
from jax import lax
from jax.sharding import PartitionSpec as P

HD = 64
NB1 = 32
NB2 = 64
CONV_TAPS = 3
CONV_DILATION = 2
norm_eps = 1e-05
masked_score = -1000000000.0


def layer_norm(inputs, norm_gain, norm_shift):
    row_mean = jnp.mean(inputs, axis=-1, keepdims=True)
    centred = inputs - row_mean
    spread = jnp.mean(centred * centred, axis=-1, keepdims=True)
    return centred * lax.rsqrt(spread + norm_eps) * norm_gain + norm_shift


def exact_gelu(inputs):
    return jax.nn.gelu(inputs, approximate=False)


def contract_rows(left_side, right_side):
    return lax.dot_general(
        left_side, right_side, (((0,), (0,)), ((), ())), preferred_element_type=jnp.float32
    )


def contract_cols(left_side, right_side):
    return lax.dot_general(
        left_side, right_side, (((1,), (1,)), ((), ())), preferred_element_type=jnp.float32
    )


def bucket_hits(pos_ids, x_ids, y_ids):
    bucket_index = lax.broadcasted_iota(jnp.int32, (NB1 + 2 * NB2, 1), 0)
    first_hit = bucket_index == pos_ids.reshape(1, -1)
    second = bucket_index == x_ids.reshape(1, -1) + NB1
    third_hit = bucket_index == y_ids.reshape(1, -1) + NB1 + NB2
    return first_hit | second | third_hit


def id_blocks(id_array, block_rows):
    page_count, row_count, col_count = id_array.shape
    return id_array.reshape(page_count * row_count // block_rows, block_rows, col_count)


def table_bias(table_rows, pos_ids, x_ids, y_ids):
    page_count, row_count, col_count = pos_ids.shape
    block_rows = math.gcd(row_count, 64)
    head_count = table_rows.shape[0]

    def one_block(pieces):
        bucket_hit = bucket_hits(pieces[0], pieces[1], pieces[2]).astype(jnp.float32)
        looked_up = jnp.dot(table_rows, bucket_hit, precision=lax.Precision.HIGHEST)
        return looked_up.astype(jnp.bfloat16).reshape(head_count, block_rows, col_count)

    blocks = lax.map(
        one_block,
        (
            id_blocks(pos_ids, block_rows),
            id_blocks(x_ids, block_rows),
            id_blocks(y_ids, block_rows),
        ),
    )
    blocks = blocks.reshape(page_count, row_count // block_rows, head_count, block_rows, col_count)
    return jnp.transpose(blocks, (0, 2, 1, 3, 4)).reshape(
        page_count, head_count, row_count, col_count
    )


def table_grad(score_grad, pos_ids, x_ids, y_ids):
    page_count, head_count, row_count, col_count = score_grad.shape
    block_rows = math.gcd(row_count, 64)
    block_count = page_count * row_count // block_rows
    grad_blocks = score_grad.reshape(
        page_count, head_count, row_count // block_rows, block_rows * col_count
    )
    grad_blocks = jnp.transpose(grad_blocks, (0, 2, 1, 3)).reshape(
        block_count, head_count, block_rows * col_count
    )

    def add_block(running, pieces):
        bucket_hit = bucket_hits(pieces[1], pieces[2], pieces[3]).astype(jnp.bfloat16)
        return (running + contract_cols(pieces[0], bucket_hit), None)

    zero_start = jnp.zeros((head_count, NB1 + 2 * NB2), jnp.float32)
    running, unused = lax.scan(
        add_block,
        zero_start,
        (
            grad_blocks,
            id_blocks(pos_ids, block_rows),
            id_blocks(x_ids, block_rows),
            id_blocks(y_ids, block_rows),
        ),
    )
    return running


def body(
    tokens,
    lang,
    page_len,
    rel_pos,
    rel_x,
    rel_y,
    lang_table,
    convolution_weight,
    conv_b,
    w_qkv,
    b_qv,
    bias_table,
    w_out,
    b_out,
    ln1_gain,
    ln1_bias,
    w_in,
    b_in,
    w_down,
    b_down,
    ln2_gain,
    ln2_bias,
    cotangent,
):
    page_count = page_len.shape[0]
    count_of_slots = rel_pos.shape[2]
    model_width = tokens.shape[1]
    local_cols = w_qkv.shape[2]
    heads_here = local_cols // HD
    total_rows = page_count * count_of_slots
    score_scale = HD ** (-0.5)
    slot_index = lax.broadcasted_iota(jnp.int32, (page_count, count_of_slots), 1)
    live_mask = slot_index < page_len[:, None]
    live_rows = live_mask.astype(jnp.float32)[:, :, None]
    key_live = live_mask[:, None, None, :]
    languages = lax.broadcasted_iota(jnp.int32, (1, lang_table.shape[0]), 1)
    lang_pick = (lang[:, None] == languages).astype(jnp.float32)
    convolution_reach = CONV_TAPS // 2 * CONV_DILATION

    def embed(tok_in, lang_weights, kernel_taps, kernel_bias):
        with_lang = (
            tok_in + jnp.dot(lang_pick, lang_weights, precision=lax.Precision.HIGHEST)[:, None, :]
        )
        padded_rows = jnp.pad(
            with_lang * live_rows, ((0, 0), (convolution_reach, convolution_reach), (0, 0))
        )
        convolution_sum = kernel_bias
        for index_of_tap in range(CONV_TAPS):
            convolution_sum = (
                convolution_sum
                + kernel_taps[index_of_tap]
                * padded_rows[
                    :, index_of_tap * CONV_DILATION : index_of_tap * CONV_DILATION + count_of_slots
                ]
            )
        return with_lang + convolution_sum

    tok_in = tokens.astype(jnp.float32).reshape(page_count, count_of_slots, model_width)
    first_pages, embed_back = jax.vjp(embed, tok_in, lang_table, convolution_weight, conv_b)
    first_in = first_pages.reshape(total_rows, model_width)
    first_low = first_in.astype(jnp.bfloat16)
    qkv_flat = w_qkv.reshape(model_width, 3 * local_cols)
    projected = jnp.dot(first_low, qkv_flat, preferred_element_type=jnp.float32).reshape(
        total_rows, 3, local_cols
    )
    head_shape = (page_count, count_of_slots, heads_here, HD)
    queries = (projected[:, 0] + b_qv[0]).astype(jnp.bfloat16).reshape(head_shape)
    key_rows = projected[:, 1].astype(jnp.bfloat16).reshape(head_shape)
    value_rows = (projected[:, 2] + b_qv[1]).astype(jnp.bfloat16).reshape(head_shape)
    row_bias = table_bias(jnp.transpose(bias_table), rel_pos, rel_x, rel_y)
    head_bias = lax.all_to_all(row_bias, "mp", split_axis=1, concat_axis=2, tiled=True)
    scores = (
        jnp.einsum("pqhd,pkhd->phqk", queries, key_rows, preferred_element_type=jnp.float32)
        * score_scale
    )
    scores = jnp.where(key_live, scores + head_bias.astype(jnp.float32), masked_score)
    top_score = jnp.max(scores, axis=-1, keepdims=True)
    exp_scores = jnp.exp(scores - top_score)
    probs_full = exp_scores / jnp.sum(exp_scores, axis=-1, keepdims=True)
    probs_low = probs_full.astype(jnp.bfloat16)
    mixed_heads = jnp.einsum(
        "phqk,pkhd->pqhd", probs_low, value_rows, preferred_element_type=jnp.float32
    )
    mixed_low = mixed_heads.astype(jnp.bfloat16).reshape(total_rows, local_cols)
    attn_part = jnp.dot(mixed_low, w_out, preferred_element_type=jnp.float32)
    attn_sum = lax.psum(attn_part.astype(jnp.bfloat16), "mp").astype(jnp.float32)
    resid_one = first_in + attn_sum + b_out
    hidden_one, norm_one_back = jax.vjp(layer_norm, resid_one, ln1_gain, ln1_bias)
    hidden_low = hidden_one.astype(jnp.bfloat16)
    pre_act = jnp.dot(hidden_low, w_in, preferred_element_type=jnp.float32) + b_in
    activation, gelu_back = jax.vjp(exact_gelu, pre_act)
    activ_low = activation.astype(jnp.bfloat16)
    ffn_part = jnp.dot(activ_low, w_down, preferred_element_type=jnp.float32)
    ffn_sum = lax.psum(ffn_part.astype(jnp.bfloat16), "mp").astype(jnp.float32)
    resid_two = hidden_one + ffn_sum + b_down
    result, norm_two_back = jax.vjp(layer_norm, resid_two, ln2_gain, ln2_bias)
    grad_two, d_ln2_gain, d_ln2_bias = norm_two_back(cotangent.astype(jnp.float32))
    d_b_down = jnp.sum(grad_two, axis=0)
    grad_ffn = grad_two.astype(jnp.bfloat16)
    d_w_down = contract_rows(activ_low, grad_ffn)
    grad_act = contract_cols(grad_ffn, w_down)
    grad_pre = gelu_back(grad_act)[0].astype(jnp.bfloat16)
    d_w_in = contract_rows(hidden_low, grad_pre)
    d_b_in = jnp.sum(grad_pre.astype(jnp.float32), axis=0)
    ffn_back = contract_cols(grad_pre, w_in)
    grad_hidden = grad_two + lax.psum(ffn_back.astype(jnp.bfloat16), "mp").astype(jnp.float32)
    grad_one, d_ln1_gain, d_ln1_bias = norm_one_back(grad_hidden)
    d_b_out = jnp.sum(grad_one, axis=0)
    grad_attn = grad_one.astype(jnp.bfloat16)
    d_w_out = contract_rows(mixed_low, grad_attn)
    grad_mixed = contract_cols(grad_attn, w_out).astype(jnp.bfloat16).reshape(head_shape)
    d_values = jnp.einsum(
        "phqk,pqhd->pkhd", probs_low, grad_mixed, preferred_element_type=jnp.float32
    ).astype(jnp.bfloat16)
    grad_probs = jnp.einsum(
        "pqhd,pkhd->phqk", grad_mixed, value_rows, preferred_element_type=jnp.float32
    )
    grad_scores = probs_full * (
        grad_probs - jnp.sum(probs_full * grad_probs, axis=-1, keepdims=True)
    )
    grad_scores = grad_scores.astype(jnp.bfloat16)
    d_queries = (
        jnp.einsum("phqk,pkhd->pqhd", grad_scores, key_rows, preferred_element_type=jnp.float32)
        * score_scale
    ).astype(jnp.bfloat16)
    d_keys = (
        jnp.einsum("phqk,pqhd->pkhd", grad_scores, queries, preferred_element_type=jnp.float32)
        * score_scale
    ).astype(jnp.bfloat16)
    grad_qkv = jnp.stack([d_queries, d_keys, d_values], axis=2).reshape(total_rows, 3 * local_cols)
    d_w_qkv = contract_rows(first_low, grad_qkv).reshape(model_width, 3, local_cols)
    grad_cols = jnp.sum(grad_qkv.astype(jnp.float32), axis=0).reshape(3, local_cols)
    d_b_qv = jnp.stack([grad_cols[0], grad_cols[2]])
    attn_back = contract_cols(grad_qkv, qkv_flat)
    grad_rows = lax.all_to_all(grad_scores, "mp", split_axis=2, concat_axis=1, tiled=True)
    table_part = jnp.transpose(table_grad(grad_rows, rel_pos, rel_x, rel_y))
    input_sum, d_bias_table = (
        lax.psum(attn_back.astype(jnp.bfloat16), "mp").astype(jnp.float32),
        lax.psum(table_part.astype(jnp.bfloat16), "mp").astype(jnp.float32),
    )
    grad_first = grad_one + input_sum
    d_tokens, d_lang_table, d_conv_w, d_conv_b = embed_back(
        grad_first.reshape(page_count, count_of_slots, model_width)
    )
    (
        d_lang_table,
        d_conv_w,
        d_conv_b,
        d_w_qkv,
        d_b_qv,
        d_bias_table,
        d_w_out,
        d_b_out,
        d_ln1_gain,
        d_ln1_bias,
        d_w_in,
        d_b_in,
        d_w_down,
        d_b_down,
        d_ln2_gain,
        d_ln2_bias,
    ) = lax.psum(
        (
            d_lang_table,
            d_conv_w,
            d_conv_b,
            d_w_qkv,
            d_b_qv,
            d_bias_table,
            d_w_out,
            d_b_out,
            d_ln1_gain,
            d_ln1_bias,
            d_w_in,
            d_b_in,
            d_w_down,
            d_b_down,
            d_ln2_gain,
            d_ln2_bias,
        ),
        "dp",
    )
    return (
        result.astype(jnp.bfloat16),
        d_tokens.reshape(total_rows, model_width).astype(jnp.bfloat16),
        d_lang_table,
        d_conv_w,
        d_conv_b,
        d_w_qkv,
        d_b_qv,
        d_bias_table,
        d_w_out,
        d_b_out,
        d_ln1_gain,
        d_ln1_bias,
        d_w_in,
        d_b_in,
        d_w_down,
        d_b_down,
        d_ln2_gain,
        d_ln2_bias,
    )


def solution(mesh):
    in_specs = (
        P("dp", None),
        P("dp"),
        P("dp"),
        P("dp", "mp", None),
        P("dp", "mp", None),
        P("dp", "mp", None),
        P(),
        P(),
        P(),
        P(None, None, "mp"),
        P(None, "mp"),
        P(),
        P("mp", None),
        P(),
        P(),
        P(),
        P(None, "mp"),
        P("mp"),
        P("mp", None),
        P(),
        P(),
        P(),
        P("dp", None),
    )
    out_specs = (
        P("dp", None),
        P("dp", None),
        P(),
        P(),
        P(),
        P(None, None, "mp"),
        P(None, "mp"),
        P(),
        P("mp", None),
        P(),
        P(),
        P(),
        P(None, "mp"),
        P("mp"),
        P("mp", None),
        P(),
        P(),
        P(),
    )
    return jax.shard_map(body, mesh=mesh, in_specs=in_specs, out_specs=out_specs, check_vma=False)
```

profile of v0, /device:TPU:0, one launch (start us, length us, event | category | flops | bytes accessed | tf_op | source)
XLA Modules:
  0.0 1170.5 jit_solution(16028194539182809648)
XLA Ops:
  7.2 153.9 %while.25 = (s32[]{:T(128)}, bf16[22,12,16,704]{3,2,1,0:T(8,128)(2,1)}, s32[22,16,704]{2,1,0:T(8,128)}, s32[22,16,704]{2,1,0:T(8,128)}, s32[22,16,704]{2,1,0:T(8,128)}, /*index=5*/f32[12,160]{1,0:T(8,128)}, s32[]{:T(128)}) while((s32[]{:T(128)}, bf16[22,12,16,704]{3,2,1,0:T(8,128)(2,1)}, s32[22,16,704]{2,1,0:T(8,128)}, ...), condition=%wide.region_1.2_spmd, body=%wide.region_0.1_spmd.sunk | while | flops 268691456 | bytes 2059873 | solution.py:62
  9.2 3.9 fusion.132
  16.2 3.9 fusion.132
  23.2 3.9 fusion.132
  30.2 3.9 fusion.132
  37.2 3.9 fusion.132
  44.2 3.9 fusion.132
  51.2 3.9 fusion.132
  58.2 3.9 fusion.132
  65.2 3.9 fusion.132
  72.1 3.9 fusion.132
  79.1 3.9 fusion.132
  86.1 3.9 fusion.132
  93.1 3.9 fusion.132
  100.1 3.9 fusion.132
  107.1 3.9 fusion.132
  114.1 3.9 fusion.132
  121.1 3.9 fusion.132
  128.1 3.9 fusion.132
  135.1 3.9 fusion.132
  142.1 3.9 fusion.132
  149.1 3.9 fusion.132
  156.1 3.9 fusion.132
  161.2 3.3 copy.111
  167.7 6.5 all-to-all-start
  175.6 3.5 fusion.91
  187.3 129.8 %all-to-all-done = bf16[2,12,176,704]{3,2,0,1:T(8,128)(2,1)} async-done(((bf16[2,12,176,704]{3,2,0,1:T(8,128)(2,1)}), bf16[2,12,176,704]{3,2,0,1:T(8,128)(2,1)}, u32[]{:S(2)}, u32[]{:S(2)}) %all-to-all-start) | async-done | bytes 5947424 | tf_op jit(solution)/shard_map/all_to_all | solution.py:176
  317.2 3.3 copy.113
  320.4 6.2 convert_bitcast_fusion
  326.6 10.5 copy.114
  337.1 14.6 %copy.115 = f32[2,3,704,704]{2,3,1,0:T(8,128)} copy(f32[2,3,704,704]{3,2,1,0:T(8,128)} %bitcast.116) | data formatting | bytes 23789568 | tf_op jit(solution)/shard_map/convert_element_type | solution.py:181
  351.7 9.5 add_select_fusion
  361.2 15.6 %fusion.94 = (f32[2,3,704]{2,1,0:T(4,128)S(1)}, f32[2,3,704,704]{2,3,1,0:T(8,128)}) fusion(f32[2,3,704,704]{2,3,1,0:T(8,128)} %add_select_fusion), kind=kOutput, calls=%fused_computation.168 | output fusion | flops 5948095 | bytes 23806464 | tf_op jit(solution)/shard_map/sub | solution.py:183
  376.8 11.9 %fusion.53 = bf16[2,704,3,64]{1,3,2,0:T(8,128)(2,1)S(1)} fusion(f32[2,704,3,64]{1,0,3,2:T(2,128)} %squeeze.24, f32[3,64]{1,0:T(4,128)S(1)} %add.278, f32[2,3,704]{2,1,0:T(4,128)S(1)} %get-tuple-element.305, f32[2,3,704,704]{2,3,1,0:T(8,128)} %add_select_fusion), kind=kOutput, calls=%fused_computation.115 | convolution fusion | flops 390370112 | bytes 13534464 | tf_op jit(solution)/shard_map/phqk,pkhd->pqhd/dot_general | solution.py:186
  392.0 87.5 %all-reduce.16.cloned.1.call-done = bf16[1408,768]{1,0:T(8,128)(2,1)} async-done(((bf16[1408,768]{1,0:T(8,128)(2,1)}), bf16[1408,768]{1,0:T(8,128)(2,1)}) %all-reduce.16.cloned.1.call-update) | async-done | bytes 2162704 | tf_op jit(solution)/shard_map/psum | solution.py:191
  479.5 3.5 fusion.89
  485.1 12.3 %multiply_convert_fusion.1 = (bf16[1408,768]{1,0:T(8,128)(2,1)S(1)}, f32[1408,768]{1,0:T(8,128)}, f32[1408,768]{1,0:T(8,128)}) fusion(f32[768]{0:T(1024)S(1)} %copy-done.50, bf16[1408,768]{1,0:T(8,128)(2,1)S(1)} %fusion.37, bf16[768,768]{1,0:T(8,128)(2,1)S(1)} %copy-done), kind=kOutput, calls=%fused_computation.69 | convolution fusion | flops 1732313088 | bytes 14158848 | tf_op jit(solution)/shard_map/dot_general | solution.py:195
  502.0 87.4 %all-reduce.18.cloned.1.call-done = bf16[1408,768]{1,0:T(8,128)(2,1)} async-done(((bf16[1408,768]{1,0:T(8,128)(2,1)}), bf16[1408,768]{1,0:T(8,128)(2,1)}) %all-reduce.18.cloned.1.call-update) | async-done | bytes 2162704 | tf_op jit(solution)/shard_map/psum | solution.py:199
  589.4 4.4 fusion.87
  600.3 3.7 convert_reduce_fusion.1
  608.6 87.5 %all-reduce.20.cloned.1.call-done = bf16[1408,768]{1,0:T(8,128)(2,1)} async-done(((bf16[1408,768]{1,0:T(8,128)(2,1)}), bf16[1408,768]{1,0:T(8,128)(2,1)}) %all-reduce.20.cloned.1.call-update) | async-done | bytes 2162704 | tf_op jit(solution)/shard_map/psum | solution.py:211
  696.1 6.6 multiply_reduce_fusion.1
  702.7 5.7 fusion.85
  712.0 10.9 multiply_reduce_fusion
  725.2 9.0 multiply_convert_fusion
  734.2 18.2 %copy.125 = bf16[2,3,704,704]{3,0,1,2:T(2,128)(2,1)} copy(bf16[2,3,704,704]{2,3,1,0:T(8,128)(2,1)} %multiply_convert_fusion) | data formatting | bytes 11894784 | tf_op jit(solution)/shard_map/convert_element_type | solution.py:226
  752.3 5.3 all-to-all-start.1
  757.6 11.4 fusion.50
  769.0 4.3 fusion.57
  773.4 4.9 fusion.56
  781.7 5.0 reshape.328
  786.7 4.9 convolution_convert_fusion.2
  791.9 5.2 fusion.96
  797.2 6.4 fusion.78
  803.7 4.0 fusion.80
  810.5 159.4 %all-reduce.22.cloned.1.call-done = bf16[1408,768]{1,0:T(8,128)(2,1)} async-done(((bf16[1408,768]{1,0:T(8,128)(2,1)}), bf16[1408,768]{1,0:T(8,128)(2,1)}) %all-reduce.22.cloned.1.call-update) | async-done | bytes 2162704 | tf_op jit(solution)/shard_map/psum | solution.py:243
  969.9 4.5 fusion.82
  977.3 5.8 multiply_reduce_fusion.3
  983.4 3.8 copy.126
  990.4 13.8 %reshape.330 = bf16[2,12,11,11264]{3,2,1,0:T(8,128)(2,1)} reshape(bf16[2,4,3,176,704]{4,3,2,1,0:T(8,128)(2,1)} %copy.127) | data formatting | bytes 11894784 | tf_op jit(solution)/shard_map/reshape | solution.py:80
  1004.2 10.4 copy.134
  1014.6 107.7 %while.26 = (s32[]{:T(128)}, f32[12,160]{1,0:T(8,128)S(1)}, bf16[22,12,11264]{2,1,0:T(8,128)(2,1)}, s32[22,16,704]{2,1,0:T(8,128)}, s32[22,16,704]{2,1,0:T(8,128...) while((s32[]{:T(128)}, f32[12,160]{1,0:T(8,128)S(1)}, bf16[22,12,11264]{2,1,0:T(8,128)(2,1)}, ...), condition=%wide.region_29.30_spmd.clone, body=%wide.region_28.29_spmd.clone.sunk | while | flops 52291328 | bytes 1051763 | solution.py:92
  1122.4 9.9 psum.156
  1132.2 23.8 %all-reduce.25 = (f32[8,768]{1,0:T(8,128)}, f32[3,768]{1,0:T(4,128)}, f32[768]{0:T(1024)}, f32[2,192]{1,0:T(2,128)}, f32[160,12]{0,1:T(8,128)}, /*index=5*/f32[7...) all-reduce(f32[8,768]{1,0:T(8,128)S(1)} %fusion.73, ...), channel_id=1, replica_groups=mesh['dp'=8,'mp'=4] {'dp'}, use_global_device_ids=true, to_apply=%region_18.19 | all-reduce | flops 16896 | bytes 131328 | tf_op jit(solution)/shard_map/psum | solution.py:267
  (488 shorter events, 234.4 us)
Async XLA Ops:
  7.2 477.9 %copy-start = (bf16[768,768]{1,0:T(8,128)(2,1)S(1)}, bf16[768,768]{1,0:T(8,128)(2,1)}, u32[]{:S(2)}) copy-start(bf16[768,768]{1,0:T(8,128)(2,1)} %param.43) | copy-start | bytes 3538948
  167.7 6.8 copy-start.39
  167.7 6.9 copy-start.45
  167.7 7.0 copy-start.49
  167.7 7.0 copy-start.51
  167.7 7.2 copy-start.9
  167.7 149.5 %all-to-all-start = ((bf16[2,12,176,704]{3,2,0,1:T(8,128)(2,1)}), bf16[2,12,176,704]{3,2,0,1:T(8,128)(2,1)}, u32[]{:S(2)}, u32[]{:S(2)}) async-start(bf16[2,12,176,704]{3,2,0,1:T(8,128)(2,1)} %copy.112), calls=%async_computation | async-start | bytes 12976128 | tf_op jit(solution)/shard_map/all_to_all | solution.py:176
  174.2 305.3 %all-reduce.16.cloned.1.call-start = ((), (), s32[]{:S(2)}) async-start(), calls=%async_computation.2 | async-start | bytes 4325376 | tf_op jit(solution)/shard_map/psum | solution.py:191
  175.5 3.6 copy-start.4
  175.6 3.5 copy-start.48
  179.1 1.7 copy-start.18
  180.7 3.3 copy-start.44
  184.6 167.1 %copy-start.12 = (bf16[2,704,3,64]{1,0,3,2:T(2,128)(2,1)}, bf16[2,704,3,64]{1,0,3,2:T(2,128)(2,1)S(1)}, u32[]{:S(2)}) copy-start(bf16[2,704,3,64]{1,0,3,2:T(2,128)(2,1)S(1)} %convert_element_type.168) | copy-start | bytes 1622020
  187.2 164.5 %copy-start.6 = (f32[2,704,3,64]{1,0,3,2:T(2,128)}, f32[2,704,3,64]{1,0,3,2:T(2,128)S(1)}, u32[]{:S(2)}) copy-start(f32[2,704,3,64]{1,0,3,2:T(2,128)S(1)} %squeeze.25) | copy-start | bytes 3244036
  187.3 164.4 %copy-start.29 = (f32[3,64]{1,0:T(4,128)}, f32[3,64]{1,0:T(4,128)S(1)}, u32[]{:S(2)}) copy-start(f32[3,64]{1,0:T(4,128)S(1)} %add.281) | copy-start | bytes 2308
  376.8 13.0 %copy-start.21 = (bf16[192,768]{1,0:T(8,128)(2,1)S(1)}, bf16[192,768]{1,0:T(8,128)(2,1)}, u32[]{:S(2)}) copy-start(bf16[192,768]{1,0:T(8,128)(2,1)} %param.39) | copy-start | bytes 884740
  388.7 90.8 %copy-start.41 = (f32[768]{0:T(1024)S(1)}, f32[768]{0:T(1024)}, u32[]{:S(2)}) copy-start(f32[768]{0:T(1024)} %param.40) | copy-start | bytes 9220
  389.8 93.2 %copy-start.13 = (bf16[1408,192]{0,1:T(8,128)(2,1)}, bf16[1408,192]{0,1:T(8,128)(2,1)S(1)}, u32[]{:S(2)}) copy-start(bf16[1408,192]{0,1:T(8,128)(2,1)S(1)} %reshape.326) | copy-start | bytes 1622020
  391.9 197.5 %all-reduce.18.cloned.1.call-start = ((), (), s32[]{:S(2)}) async-start(), calls=%async_computation.3 | async-start | bytes 4325376 | tf_op jit(solution)/shard_map/psum | solution.py:199
  483.0 2.1 copy-start.2
  483.7 1.4 copy-start.50
  485.1 13.6 %copy-start.46 = (bf16[768,768]{1,0:T(8,128)(2,1)S(1)}, bf16[768,768]{1,0:T(8,128)(2,1)}, u32[]{:S(2)}) copy-start(bf16[768,768]{1,0:T(8,128)(2,1)} %param.45) | copy-start | bytes 3538948
  497.4 1.3 copy-start.53
  498.7 90.7 %copy-start.40 = (f32[768]{0:T(1024)S(1)}, f32[768]{0:T(1024)}, u32[]{:S(2)}) copy-start(f32[768]{0:T(1024)} %param.46) | copy-start | bytes 9220
  501.9 194.1 %all-reduce.20.cloned.1.call-start = ((), (), s32[]{:S(2)}) async-start(), calls=%async_computation.4 | async-start | bytes 4325376 | tf_op jit(solution)/shard_map/psum | solution.py:211
  593.7 1.6 copy-start.8
  593.8 1.6 copy-start.38
  594.4 2.7 copy-start.42
  595.4 4.9 slice-start.6
  595.4 4.9 slice-start.8
  597.0 3.2 copy-start.47
  597.1 3.2 slice-start.7
  597.1 3.2 slice-start.9
  600.2 3.8 copy-start.5
  604.0 1.3 copy-start.17
  696.1 6.6 copy-start.11
  702.7 7.8 copy-start.22
  708.4 2.1 copy-start.3
  712.0 10.9 slice-start
  712.0 12.0 %slice-start.1 = ((s8[12976128]{0:T(1024)(128)(4,1)}), s8[4194304]{0:T(1024)(128)(4,1)S(1)}, s32[]{:S(2)}) async-start(s8[12976128]{0:T(1024)(128)(4,1)} %bitcast.117), calls=%async_computation.8 | async-start | bytes 8388608
  712.0 13.2 %slice-start.2 = ((s8[12976128]{0:T(1024)(128)(4,1)}), s8[4194304]{0:T(1024)(128)(4,1)S(1)}, s32[]{:S(2)}) async-start(s8[12976128]{0:T(1024)(128)(4,1)} %bitcast.117), calls=%async_computation.9 | async-start | bytes 8388608
  712.0 13.2 %slice-start.3 = ((s8[12976128]{0:T(1024)(128)(4,1)}), s8[393216]{0:T(1024)(128)(4,1)S(1)}, s32[]{:S(2)}) async-start(s8[12976128]{0:T(1024)(128)(4,1)} %bitcast.117), calls=%async_computation.10 | async-start | bytes 786432
  752.3 231.1 %all-to-all-start.1 = ((bf16[2,3,704,704]{3,0,1,2:T(2,128)(2,1)}), bf16[2,3,704,704]{3,0,1,2:T(2,128)(2,1)}, u32[]{:S(2)}, u32[]{:S(2)}) async-start(bf16[2,3,704,704]{3,0,1,2:T(2,128)(2,1)} %copy.125), calls=%async_computation.1 | async-start | bytes 12976128 | tf_op jit(solution)/shard_map/all_to_all | solution.py:240
  757.6 212.4 %all-reduce.22.cloned.1.call-start = ((), (), s32[]{:S(2)}) async-start(), calls=%async_computation.5 | async-start | bytes 4325376 | tf_op jit(solution)/shard_map/psum | solution.py:243
  769.0 4.3 copy-start.7
  769.0 4.3 copy-start.30
  773.4 4.9 copy-start.23
  786.7 5.1 copy-start.25
  791.6 364.4 %all-reduce.24.cloned.1.call-start = ((), (), s32[]{:S(2)}) async-start(), calls=%async_computation.6 | async-start | bytes 14155776 | tf_op jit(solution)/shard_map/psum | solution.py:267
  791.9 5.2 copy-start.54
  797.2 6.5 copy-start.14
  803.5 4.1 copy-start.19
  803.7 4.0 copy-start.20
  810.4 159.5 %copy-start.10 = (bf16[1408,768]{1,0:T(8,128)(2,1)S(1)}, bf16[1408,768]{1,0:T(8,128)(2,1)}, u32[]{:S(2)}) copy-start(bf16[1408,768]{1,0:T(8,128)(2,1)} %param.27) | copy-start | bytes 6488068
  810.4 159.5 %copy-start.28 = (f32[2,768]{1,0:T(2,128)S(1)}, f32[2,768]{1,0:T(2,128)}, u32[]{:S(2)}) copy-start(f32[2,768]{1,0:T(2,128)} %copy-done.27) | copy-start | bytes 18436
  810.5 164.0 %copy-start.32 = (f32[768]{0:T(1024)S(1)}, f32[768]{0:T(1024)}, u32[]{:S(2)}) copy-start(f32[768]{0:T(1024)} %copy-done.31) | copy-start | bytes 9220
  810.5 164.0 %copy-start.34 = (f32[768]{0:T(1024)S(1)}, f32[768]{0:T(1024)}, u32[]{:S(2)}) copy-start(f32[768]{0:T(1024)} %copy-done.33) | copy-start | bytes 9220
  810.5 164.0 %copy-start.36 = (f32[768]{0:T(1024)S(1)}, f32[768]{0:T(1024)}, u32[]{:S(2)}) copy-start(f32[768]{0:T(1024)} %copy-done.35) | copy-start | bytes 9220
  969.9 7.4 slice-start.4
  974.5 2.8 slice-start.5
  977.3 5.8 copy-start.52
  1156.0 5.0 copy-start.16
  1156.0 6.4 copy-start.15
  1159.0 4.8 copy-start.1
  (8 other events, 6.8 us)
Sparse Core Ops, SparseCore 0:
  392.0 87.3 all-reduce.15
  502.1 87.2 all-reduce.17
  608.7 87.2 all-reduce.19
  791.7 178.1 all-reduce.21
  974.6 111.6 all-reduce.23
where the time goes:
time: 1180 us; the launch traced here: 1170 us
  waiting for transfers between devices  552 us (47%)
  matrix products  256 us (22%)
  local copies, waits for them, and re-layouts  189 us (16%)
  other arithmetic  113 us (10%)
  blocking collectives  33.6 us (3%)
  between operations  14.8 us (1%)
  starting transfers between devices  12.4 us (1%)
    psum x1, waiting for transfers between devices, body(): lax.psum(attn_back.astype(jnp.bfloat16), 'mp').astype(jnp.float32)  159 us
    all_to_all x1, waiting for transfers between devices, body(): lax.all_to_all(row_bias, 'mp', split_axis=1, concat_axis=2, tiled=True)  130 us
    psum x1, waiting for transfers between devices, body(): lax.psum(attn_part.astype(jnp.bfloat16), 'mp').astype(jnp.float32)  87.5 us
    psum x1, waiting for transfers between devices, body(): lax.psum(ffn_back.astype(jnp.bfloat16), 'mp').astype(jnp.float32)  87.5 us
    psum x1, waiting for transfers between devices, body(): ffn_sum = lax.psum(ffn_part.astype(jnp.bfloat16), 'mp').astype(jnp.float32)  87.4 us
    dot_general x22, matrix products, one_block(): looked_up = jnp.dot(table_rows, bucket_hit, precision=lax.Precision.HIGHEST)  86.8 us
    dot_general x26, matrix products, contract_cols(): lax.dot_general(left_side, right_side, (((1,), (1,)), ((), ())), preferre...  78.2 us
    add x44, other arithmetic, bucket_hits(): third_hit = bucket_index == y_ids.reshape(1, -1) + NB1 + NB2  36.8 us
  transfers between devices with their start and end apart: 7, of which 5 were waited for; matrix products, arithmetic and copies ran while one was open for 19% of the time, Pallas kernels for 0%

commit v1 on v0

--- a/solution.py
+++ b/solution.py
@@ -240,7 +240,7 @@
     grad_rows = lax.all_to_all(grad_scores, "mp", split_axis=2, concat_axis=1, tiled=True)
     table_part = jnp.transpose(table_grad(grad_rows, rel_pos, rel_x, rel_y))
     input_sum, d_bias_table = (
-        lax.psum(attn_back.astype(jnp.bfloat16), "mp").astype(jnp.float32),
+        jnp.sum(lax.all_gather(attn_back.astype(jnp.bfloat16), "mp"), axis=0).astype(jnp.float32),
         lax.psum(table_part.astype(jnp.bfloat16), "mp").astype(jnp.float32),
     )
     grad_first = grad_one + input_sum

time: 1180 us -> 1270 us (1.076)
  waiting for transfers between devices: 552 us -> 642 us
    all_to_all x1, waiting for transfers between devices: 0.01 us -> 249 us  [body(): lax.all_to_all(grad_scores, 'mp', split_axis=2, concat_axis=1, tiled=True)]
    psum x1 -> x0, waiting for transfers between devices: 159 us -> none  [body(): lax.psum(attn_back.astype(jnp.bfloat16), 'mp').astype(jnp.float32)]
    unnamed x135 -> x153, local copies, waits for them, and re-layouts: 26.6 us -> 25.2 us
  transfers between devices with their start and end apart: 7 -> 7, of which waited for: 5 -> 5; matrix products, arithmetic and copies ran while one was open for 19% -> 16% of each run, Pallas kernels for 0% -> 0%
where the time goes in v1:
time: 1270 us; the launch traced here: 1260 us
  waiting for transfers between devices  642 us (51%)
  matrix products  251 us (20%)
  local copies, waits for them, and re-layouts  186 us (15%)
  other arithmetic  118 us (9%)
  blocking collectives  33.4 us (3%)
  between operations  15.2 us (1%)
    all_to_all x1, waiting for transfers between devices, body(): lax.all_to_all(grad_scores, 'mp', split_axis=2, concat_axis=1, tiled=True)  249 us
    all_to_all x1, waiting for transfers between devices, body(): lax.all_to_all(row_bias, 'mp', split_axis=1, concat_axis=2, tiled=True)  130 us
    psum x1, waiting for transfers between devices, body(): lax.psum(attn_part.astype(jnp.bfloat16), 'mp').astype(jnp.float32)  87.5 us
    psum x1, waiting for transfers between devices, body(): lax.psum(ffn_back.astype(jnp.bfloat16), 'mp').astype(jnp.float32)  87.4 us
    psum x1, waiting for transfers between devices, body(): ffn_sum = lax.psum(ffn_part.astype(jnp.bfloat16), 'mp').astype(jnp.float32)  87.4 us
    dot_general x22, matrix products, one_block(): looked_up = jnp.dot(table_rows, bucket_hit, precision=lax.Precision.HIGHEST)  86.8 us
    dot_general x26, matrix products, contract_cols(): lax.dot_general(left_side, right_side, (((1,), (1,)), ((), ())), preferre...  78.6 us
    add x44, other arithmetic, bucket_hits(): third_hit = bucket_index == y_ids.reshape(1, -1) + NB1 + NB2  36.8 us
  transfers between devices with their start and end apart: 7, of which 5 were waited for; matrix products, arithmetic and copies ran while one was open for 16% of the time, Pallas kernels for 0%

profile of v1, /device:TPU:0, one launch (start us, length us, event | category | flops | bytes accessed | tf_op | source)
XLA Modules:
  0.0 1259.4 jit_solution(7807050166041728749)
XLA Ops:
  7.2 153.8 %while.25 = (s32[]{:T(128)}, bf16[22,12,16,704]{3,2,1,0:T(8,128)(2,1)}, s32[22,16,704]{2,1,0:T(8,128)}, s32[22,16,704]{2,1,0:T(8,128)}, s32[22,16,704]{2,1,0:T(8,128)}, /*index=5*/f32[12,160]{1,0:T(8,128)}, s32[]{:T(128)}) while((s32[]{:T(128)}, bf16[22,12,16,704]{3,2,1,0:T(8,128)(2,1)}, s32[22,16,704]{2,1,0:T(8,128)}, ...), condition=%wide.region_1.2_spmd, body=%wide.region_0.1_spmd.sunk | while | flops 268691456 | bytes 2059873 | solution.py:62
  9.2 3.9 fusion.132
  16.2 3.9 fusion.132
  23.2 3.9 fusion.132
  30.2 3.9 fusion.132
  37.2 3.9 fusion.132
  44.1 3.9 fusion.132
  51.1 3.9 fusion.132
  58.1 3.9 fusion.132
  65.1 3.9 fusion.132
  72.1 3.9 fusion.132
  79.1 3.9 fusion.132
  86.1 3.9 fusion.132
  93.1 3.9 fusion.132
  100.1 3.9 fusion.132
  107.0 3.9 fusion.132
  114.0 3.9 fusion.132
  121.0 3.9 fusion.132
  128.0 3.9 fusion.132
  135.0 3.9 fusion.132
  141.9 3.9 fusion.132
  148.9 3.9 fusion.132
  155.9 3.9 fusion.132
  161.0 3.3 copy.111
  164.2 3.3 copy.112
  167.5 6.5 all-to-all-start
  175.6 3.5 fusion.91
  187.1 130.0 %all-to-all-done = bf16[2,12,176,704]{3,2,0,1:T(8,128)(2,1)} async-done(((bf16[2,12,176,704]{3,2,0,1:T(8,128)(2,1)}), bf16[2,12,176,704]{3,2,0,1:T(8,128)(2,1)}, u32[]{:S(2)}, u32[]{:S(2)}) %all-to-all-start) | async-done | bytes 5947424 | tf_op jit(solution)/shard_map/all_to_all | solution.py:176
  317.0 3.3 copy.113
  320.3 6.2 convert_bitcast_fusion
  326.5 10.5 copy.114
  337.0 14.7 %copy.115 = f32[2,3,704,704]{2,3,1,0:T(8,128)} copy(f32[2,3,704,704]{3,2,1,0:T(8,128)} %bitcast.117) | data formatting | bytes 23789568 | tf_op jit(solution)/shard_map/convert_element_type | solution.py:181
  351.7 9.1 add_select_fusion
  360.7 16.2 %fusion.94 = (f32[2,3,704]{2,1,0:T(4,128)}, f32[2,3,704,704]{2,3,1,0:T(8,128)}) fusion(f32[2,3,704,704]{2,3,1,0:T(8,128)} %add_select_fusion), kind=kOutput, calls=%fused_computation.168 | output fusion | flops 5948095 | bytes 23806464 | tf_op jit(solution)/shard_map/sub | solution.py:183
  376.9 11.9 fusion.53
  392.4 3.3 convolution_convert_fusion.1
  395.8 87.5 %all-reduce.15.cloned.1.call-done = bf16[1408,768]{1,0:T(8,128)(2,1)} async-done(((bf16[1408,768]{1,0:T(8,128)(2,1)}), bf16[1408,768]{1,0:T(8,128)(2,1)}) %all-reduce.15.cloned.1.call-update) | async-done | bytes 2162704 | tf_op jit(solution)/shard_map/psum | solution.py:191
  483.3 3.5 fusion.89
  488.8 12.3 multiply_convert_fusion.1
  505.8 87.4 %all-reduce.17.cloned.1.call-done = bf16[1408,768]{1,0:T(8,128)(2,1)} async-done(((bf16[1408,768]{1,0:T(8,128)(2,1)}), bf16[1408,768]{1,0:T(8,128)(2,1)}) %all-reduce.17.cloned.1.call-update) | async-done | bytes 2162704 | tf_op jit(solution)/shard_map/psum | solution.py:199
  593.2 4.4 fusion.87
  604.6 4.4 convert_reduce_fusion.1
  613.7 87.4 %all-reduce.19.cloned.1.call-done = bf16[1408,768]{1,0:T(8,128)(2,1)} async-done(((bf16[1408,768]{1,0:T(8,128)(2,1)}), bf16[1408,768]{1,0:T(8,128)(2,1)}) %all-reduce.19.cloned.1.call-update) | async-done | bytes 2162704 | tf_op jit(solution)/shard_map/psum | solution.py:211
  701.1 7.2 multiply_reduce_fusion.1
  708.3 5.7 fusion.85
  717.5 11.3 fusion.50
  728.8 11.8 multiply_reduce_fusion
  741.7 6.1 multiply_convert_fusion
  755.7 4.7 convolution_convert_fusion.2
  760.4 18.4 %copy.125 = bf16[2,3,704,704]{3,0,1,2:T(2,128)(2,1)} copy(bf16[2,3,704,704]{2,3,1,0:T(8,128)(2,1)} %copy-done.3) | data formatting | bytes 11894784 | tf_op jit(solution)/shard_map/convert_element_type | solution.py:226
  778.8 5.4 all-to-all-start.1
  784.5 5.2 fusion.96
  789.8 6.0 fusion.78
  795.9 3.9 fusion.80
  802.7 249.2 %all-to-all-done.1 = bf16[2,3,704,704]{3,0,1,2:T(2,128)(2,1)} async-done(((bf16[2,3,704,704]{3,0,1,2:T(2,128)(2,1)}), bf16[2,3,704,704]{3,0,1,2:T(2,128)(2,1)}, u32[]{:S(2)}, u32[]{:S(2)}) %all-to-all-start.1) | async-done | bytes 5947424 | tf_op jit(solution)/shard_map/all_to_all | solution.py:240
  1051.8 4.0 copy.126
  1059.0 14.0 %reshape.330 = bf16[2,12,11,11264]{3,2,1,0:T(8,128)(2,1)} reshape(bf16[2,4,3,176,704]{4,3,2,1,0:T(8,128)(2,1)} %copy.127) | data formatting | bytes 11894784 | tf_op jit(solution)/shard_map/reshape | solution.py:80
  1073.0 10.4 copy.134
  1083.4 107.6 %while.26 = (s32[]{:T(128)}, f32[12,160]{1,0:T(8,128)S(1)}, bf16[22,12,11264]{2,1,0:T(8,128)(2,1)}, s32[22,16,704]{2,1,0:T(8,128)}, s32[22,16,704]{2,1,0:T(8,128...) while((s32[]{:T(128)}, f32[12,160]{1,0:T(8,128)S(1)}, bf16[22,12,11264]{2,1,0:T(8,128)(2,1)}, ...), condition=%wide.region_29.30_spmd.clone, body=%wide.region_28.29_spmd.clone.sunk | while | flops 52291328 | bytes 1051763 | solution.py:92
  1191.0 9.4 psum.148
  1200.4 6.8 reduce_sum.232
  1207.3 4.5 fusion.82
  1214.7 5.5 multiply_reduce_fusion.3
  1220.6 24.0 %all-reduce.22 = (f32[8,768]{1,0:T(8,128)}, f32[3,768]{1,0:T(4,128)}, f32[768]{0:T(1024)}, f32[2,192]{1,0:T(2,128)}, f32[160,12]{0,1:T(8,128)}, /*index=5*/f32[7...) all-reduce(f32[8,768]{1,0:T(8,128)S(1)} %fusion.73, ...), channel_id=1, replica_groups=mesh['dp'=8,'mp'=4] {'dp'}, use_global_device_ids=true, to_apply=%region_18.19 | all-reduce | flops 16896 | bytes 131328 | tf_op jit(solution)/shard_map/psum | solution.py:267
  (507 shorter events, 234.9 us)
Async XLA Ops:
  7.2 481.6 %copy-start = (bf16[768,768]{1,0:T(8,128)(2,1)S(1)}, bf16[768,768]{1,0:T(8,128)(2,1)}, u32[]{:S(2)}) copy-start(bf16[768,768]{1,0:T(8,128)(2,1)} %param.43) | copy-start | bytes 3538948
  167.5 7.0 copy-start.45
  167.5 7.0 copy-start.53
  167.5 7.2 copy-start.58
  167.5 7.2 copy-start.60
  167.5 7.4 copy-start.10
  167.5 149.5 %all-to-all-start = ((bf16[2,12,176,704]{3,2,0,1:T(8,128)(2,1)}), bf16[2,12,176,704]{3,2,0,1:T(8,128)(2,1)}, u32[]{:S(2)}, u32[]{:S(2)}) async-start(bf16[2,12,176,704]{3,2,0,1:T(8,128)(2,1)} %copy.112), calls=%async_computation | async-start | bytes 12976128 | tf_op jit(solution)/shard_map/all_to_all | solution.py:176
  174.0 309.2 %all-reduce.15.cloned.1.call-start = ((), (), s32[]{:S(2)}) async-start(), calls=%async_computation.2 | async-start | bytes 4325376 | tf_op jit(solution)/shard_map/psum | solution.py:191
  175.5 3.5 copy-start.5
  175.6 3.5 copy-start.56
  180.6 3.3 copy-start.52
  184.0 192.9 %copy-start.51 = (f32[3,64]{1,0:T(4,128)}, f32[3,64]{1,0:T(4,128)S(1)}, u32[]{:S(2)}) copy-start(f32[3,64]{1,0:T(4,128)S(1)} %add.276) | copy-start | bytes 2308
  187.1 164.6 %copy-start.30 = (f32[3,64]{1,0:T(4,128)}, f32[3,64]{1,0:T(4,128)S(1)}, u32[]{:S(2)}) copy-start(f32[3,64]{1,0:T(4,128)S(1)} %add.279) | copy-start | bytes 2308
  388.8 94.4 %copy-start.47 = (f32[768]{0:T(1024)S(1)}, f32[768]{0:T(1024)}, u32[]{:S(2)}) copy-start(f32[768]{0:T(1024)} %param.40) | copy-start | bytes 9220
  392.4 94.4 %copy-start.13 = (bf16[1408,192]{0,1:T(8,128)(2,1)}, bf16[1408,192]{0,1:T(8,128)(2,1)S(1)}, u32[]{:S(2)}) copy-start(bf16[1408,192]{0,1:T(8,128)(2,1)S(1)} %reshape.326) | copy-start | bytes 1622020
  395.7 197.5 %all-reduce.17.cloned.1.call-start = ((), (), s32[]{:S(2)}) async-start(), calls=%async_computation.3 | async-start | bytes 4325376 | tf_op jit(solution)/shard_map/psum | solution.py:199
  488.8 12.4 copy-start.7
  488.8 13.7 %copy-start.54 = (bf16[768,768]{1,0:T(8,128)(2,1)S(1)}, bf16[768,768]{1,0:T(8,128)(2,1)}, u32[]{:S(2)}) copy-start(bf16[768,768]{1,0:T(8,128)(2,1)} %param.45) | copy-start | bytes 3538948
  502.5 90.7 %copy-start.46 = (f32[768]{0:T(1024)S(1)}, f32[768]{0:T(1024)}, u32[]{:S(2)}) copy-start(f32[768]{0:T(1024)} %param.46) | copy-start | bytes 9220
  505.7 195.3 %all-reduce.19.cloned.1.call-start = ((), (), s32[]{:S(2)}) async-start(), calls=%async_computation.4 | async-start | bytes 4325376 | tf_op jit(solution)/shard_map/psum | solution.py:211
  598.2 3.2 copy-start.48
  599.2 5.4 slice-start.6
  599.2 5.4 slice-start.8
  601.4 3.2 copy-start.55
  601.4 3.2 slice-start.7
  601.4 3.2 slice-start.9
  604.6 4.4 copy-start.6
  613.6 586.8 %all-gather.3.cloned.1.call-start = ((), (), s32[]{:S(2)}) async-start(), calls=%async_computation.5 | async-start | bytes 10813440 | tf_op jit(solution)/shard_map/all_gather | solution.py:243
  701.1 7.2 copy-start.12
  708.3 7.7 copy-start.21
  717.5 11.3 copy-start.22
  728.8 11.8 slice-start
  728.8 11.8 slice-start.1
  728.8 12.9 %slice-start.2 = ((s8[12976128]{0:T(1024)(128)(4,1)}), s8[4194304]{0:T(1024)(128)(4,1)S(1)}, s32[]{:S(2)}) async-start(s8[12976128]{0:T(1024)(128)(4,1)} %bitcast.118), calls=%async_computation.9 | async-start | bytes 8388608
  728.8 12.9 %slice-start.3 = ((s8[12976128]{0:T(1024)(128)(4,1)}), s8[393216]{0:T(1024)(128)(4,1)S(1)}, s32[]{:S(2)}) async-start(s8[12976128]{0:T(1024)(128)(4,1)} %bitcast.118), calls=%async_computation.10 | async-start | bytes 786432
  728.8 12.9 %copy-start.26 = (f32[2,3,704]{2,1,0:T(4,128)S(1)}, f32[2,3,704]{2,1,0:T(4,128)}, u32[]{:S(2)}) copy-start(f32[2,3,704]{2,1,0:T(4,128)} %get-tuple-element.305) | copy-start | bytes 50692
  741.7 6.1 copy-start.31
  747.8 3.2 copy-start.3
  751.4 4.3 copy-start.57
  778.8 5.7 copy-start.25
  778.8 5.8 copy-start.8
  778.8 273.1 %all-to-all-start.1 = ((bf16[2,3,704,704]{3,0,1,2:T(2,128)(2,1)}), bf16[2,3,704,704]{3,0,1,2:T(2,128)(2,1)}, u32[]{:S(2)}, u32[]{:S(2)}) async-start(bf16[2,3,704,704]{3,0,1,2:T(2,128)(2,1)} %copy.125), calls=%async_computation.1 | async-start | bytes 12976128 | tf_op jit(solution)/shard_map/all_to_all | solution.py:240
  784.2 460.5 %all-reduce.21.cloned.1.call-start = ((), (), s32[]{:S(2)}) async-start(), calls=%async_computation.6 | async-start | bytes 14155776 | tf_op jit(solution)/shard_map/psum | solution.py:267
  784.5 5.2 copy-start.63
  789.8 6.1 copy-start.14
  795.7 4.1 copy-start.19
  795.9 4.0 copy-start.20
  1200.4 6.8 copy-start.11
  1200.4 6.8 copy-start.29
  1207.2 4.5 copy-start.33
  1207.2 4.5 copy-start.35
  1207.3 4.5 copy-start.37
  1207.3 7.4 slice-start.4
  1211.8 2.8 slice-start.5
  1214.6 5.6 copy-start.61
  1214.6 5.9 copy-start.39
  1214.7 5.9 copy-start.40
  1214.7 5.9 copy-start.41
  1214.7 5.9 copy-start.43
  1214.7 5.9 copy-start.44
  1214.7 5.9 copy-start.49
  1244.7 5.0 copy-start.16
  1244.7 6.4 copy-start.15
  1247.6 4.8 copy-start.1
  (17 other events, 20.9 us)
Sparse Core Ops, SparseCore 0:
  395.8 87.3 all-reduce.14
  505.9 87.2 all-reduce.16
  613.7 87.2 all-reduce.18
  760.5 285.5 all-gather.2
  1050.7 110.7 all-reduce.20
